TPU v7x, 32 devices: a whole 2x2x4 slice. The times are simulated.
32 devices in a mesh: seq: 4 (over x, core), chan: 8 (over z, y).
Axes of the slice: x: 2, y: 2, z: 4, core: 2. Of those that a mesh axis runs over, the one named last changes fastest.
Arguments:
- d_out: bfloat16 [2048, 8192], P('seq', 'chan'), may hold values from -6 to 6
- w_out: bfloat16 [1024, 8192], P('chan'), may hold values from -0.0625 to 0.0625
- gate: bfloat16 [2048, 1024], P('seq', 'chan'), may hold values from -6 to 6
- inner: bfloat16 [2048, 1024], P('seq', 'chan'), may hold values from -0.125 to 0.125
- filt: bfloat16 [2048, 1024], P('seq', 'chan'), may hold values from -4 to 4
Outputs:
- grad_inner: bfloat16 [2048, 1024], P('seq', 'chan')
- grad_filter: float32 [2048, 1024], P('seq', 'chan')
All inputs are finite; a program needn't handle non-finite values.
Results may differ from a plain program's by a relative error of at most 0.005.
Values may be sent and summed in bfloat16 or wider, within the bound.
No kernel may reach another device: no remote copies, remote signals or barrier semaphores. Data moves between devices by JAX's collectives and lax.ppermute only.
A program may use at most 64 MiB of HBM per device.

v0:
```python
import math
import jax
import jax.numpy as jnp
from jax import lax
from jax.sharding import PartitionSpec as P

SUBS = 4


def spread(block, axis, holder):
    block = jnp.where(lax.axis_index(axis) == holder, block, jnp.zeros_like(block))
    return lax.psum(block, axis)


def shifted(block, axis, distance):
    devices = range(lax.axis_size(axis))
    route = [(i - distance, i) for i in devices if i - distance in devices]
    return lax.ppermute(block, axis, route)


def split_pair(matrix_in):
    upper = lax.optimization_barrier(matrix_in.astype(jnp.bfloat16))
    lower = (matrix_in - upper.astype(jnp.float32)).astype(jnp.bfloat16)
    return (upper, lower)


def body(d_out, w_out, gate, inner, filt):
    block_rows, channels = gate.shape
    sub_rows = block_rows // SUBS
    size_n = 2 * sub_rows
    seq_count = lax.axis_size("seq")
    grad_gated = jnp.einsum(
        "td,cd->tc",
        lax.all_gather(d_out, "chan", axis=1, tiled=True),
        w_out,
        preferred_element_type=jnp.float32,
    )
    grad_conv = (gate.astype(jnp.float32) * grad_gated).astype(jnp.bfloat16)
    index_row = jnp.arange(sub_rows, dtype=jnp.int32)
    angles = (index_row[:, None] * index_row[None, :] % size_n).astype(jnp.float32) * (
        2.0 * math.pi / size_n
    )
    alternate = (1 - 2 * (index_row % 2)).astype(jnp.float32)
    sine_part = (-jnp.sin(angles)).at[0].set(alternate)
    forward_upper, forward_lower = split_pair(jnp.concatenate([jnp.cos(angles), sine_part], axis=0))
    weights = jnp.where(index_row == 0, 1.0, 2.0).astype(jnp.float32)[None, :] / size_n
    inverse_sines = (-2.0 * jnp.sin(angles) / size_n).at[:, 0].set(alternate / size_n)
    inverse_matrix = jnp.concatenate([jnp.cos(angles) * weights, inverse_sines], axis=1)
    nyquist_sign = jnp.full((1,), float(1 - 2 * (sub_rows % 2)), jnp.float32)
    parity = jnp.concatenate([alternate, nyquist_sign, alternate[1:]])[:, None]
    conj_sign = jnp.concatenate(
        [jnp.ones((sub_rows + 1,), jnp.float32), -jnp.ones((sub_rows - 1,), jnp.float32)]
    )[:, None]
    keep_rows = (index_row > 0).astype(jnp.float32)[:, None]

    def transform(stacked):
        rows_data = stacked.reshape(-1, sub_rows, channels)
        spectra = jnp.einsum(
            "fs,ksc->kfc", forward_upper, rows_data, preferred_element_type=jnp.float32
        )
        spectra = spectra + jnp.einsum(
            "fs,ksc->kfc", forward_lower, rows_data, preferred_element_type=jnp.float32
        )
        return spectra.reshape(stacked.shape[0], SUBS, size_n, channels)

    def pair_sum(grad_spec, lag_stack, offset):
        later_spec = lax.slice_in_dim(lag_stack, offset + 1, offset + 1 + SUBS, axis=1)
        earlier = lax.slice_in_dim(lag_stack, offset, offset + SUBS, axis=1)
        factor = conj_sign * (later_spec + parity * earlier)
        grad_real = grad_spec[None, :, :sub_rows]
        grad_imag = grad_spec[None, :, sub_rows:]
        coef_real = factor[:, :, :sub_rows]
        coef_imag = factor[:, :, sub_rows:]
        imag_product = grad_imag * coef_imag
        product_real = grad_real * coef_real - keep_rows * imag_product
        product_imag = (
            keep_rows * (grad_real * coef_imag + grad_imag * coef_real)
            + (1.0 - keep_rows) * imag_product
        )
        return jnp.concatenate(
            [jnp.sum(product_real, axis=1), jnp.sum(product_imag, axis=1)], axis=1
        )

    def fetch_blocks(loop_step, grad_block):
        return (grad_block, spread(jnp.stack([filt, inner]), "seq", loop_step))

    def move_block(grad_block):
        return shifted(grad_block, "seq", -1)

    def contribute(loop_step, grad_block, previous, totals):
        grad_now, lag_pair = fetch_blocks(loop_step, grad_block)
        spectra = transform(jnp.concatenate([grad_now[None], lag_pair], axis=0))
        current = spectra[1:]
        lag_stack = jnp.concatenate([previous, current], axis=1)
        pair_terms = jnp.stack(
            [pair_sum(spectra[0], lag_stack, SUBS - 1 - which) for which in range(SUBS)], axis=1
        )
        return (current, totals + pair_terms)

    previous = jnp.zeros((2, SUBS, size_n, channels), jnp.float32)
    totals = jnp.zeros((2, SUBS, size_n, channels), jnp.float32)
    previous, totals = contribute(jnp.int32(0), grad_conv, previous, totals)

    def advance(loop_step, loop_carry):
        grad_block, previous, totals = loop_carry
        grad_block = move_block(grad_block)
        previous, totals = contribute(loop_step, grad_block, previous, totals)
        return (grad_block, previous, totals)

    loop_carry = lax.fori_loop(1, seq_count, advance, (grad_conv, previous, totals))
    spectra_out = loop_carry[2].reshape(2 * SUBS, size_n, channels)
    values = jnp.einsum(
        "nf,kfc->knc",
        inverse_matrix,
        spectra_out,
        precision=lax.Precision.HIGHEST,
        preferred_element_type=jnp.float32,
    )
    values = values.reshape(2, block_rows, channels)
    return (values[0].astype(jnp.bfloat16), values[1])


def solution(mesh):
    placed = (
        P("seq", "chan"),
        P("chan", None),
        P("seq", "chan"),
        P("seq", "chan"),
        P("seq", "chan"),
    )
    return jax.shard_map(
        body,
        mesh=mesh,
        in_specs=placed,
        out_specs=(P("seq", "chan"), P("seq", "chan")),
        check_vma=False,
    )
```

profile of v0, /device:TPU:0, one launch (start us, length us, event | category | flops | bytes accessed | tf_op | source)
XLA Modules:
  0.0 287.5 jit_solution(11338532694955231238)
XLA Ops:
  8.8 1.7 pad_maximum_fusion.4
  12.1 0.9 broadcast_multiply_fusion.1
  14.7 123.5 %all-gather.2.cloned.1.call-done = bf16[512,8192]{1,0:T(8,128)(2,1)} async-done(((bf16[512,1024]{1,0:T(8,128)(2,1)}), bf16[512,8192]{1,0:T(8,128)(2,1)}) %all-gather.2.cloned.1.call-update) | async-done | bytes 8388624 | tf_op jit(solution)/shard_map/all_gather | solution.py:34
  138.2 5.7 %fusion.11 = bf16[512,128]{1,0:T(8,128)(2,1)S(1)} fusion(bf16[512,8192]{1,0:T(8,128)(2,1)} %all-gather.2.cloned.1.call-done, bf16[128,8192]{1,0:T(8,128)(2,1)S(1)} %copy-done, bf16[512,128]{1,0:T(8,128)(2,1)S(1)} %copy-done.11), kind=kOutput, calls=%fused_computation.46 | convolution fusion | flops 1073938432 | bytes 10747904 | tf_op jit(solution)/shard_map/td,cd->tc/dot_general | solution.py:32
  144.0 1.0 pad_maximum_fusion.3
  147.0 0.8 subtract_reduce_fusion.5
  148.0 127.6 %while.23 = (s32[]{:T(128)}, bf16[512,128]{1,0:T(8,128)(2,1)}, f32[2,4,256,128]{2,3,1,0:T(8,128)}, f32[2,4,256,128]{2,3,0,1:T(8,128)S(1)}, bf16[2,512,128]{2,1,0...) while((s32[]{:T(128)}, bf16[512,128]{1,0:T(8,128)(2,1)}, ...), condition=%wide.region_19.20_spmd.clone.clone, body=%wide.region_9.19_spmd.clone.clone.sunk | while | flops 213975680 | bytes 36311328 | solution.py:110
  148.1 1.3 collective-permute-start
  150.2 1.4 collective-permute-done
  151.6 30.7 %all-reduce.6.cloned.1.call-done = bf16[2,512,128]{2,1,0:T(8,128)(2,1)} async-done(((bf16[2,512,128]{2,1,0:T(8,128)(2,1)}), bf16[2,512,128]{2,1,0:T(8,128)(2,1)}) %all-reduce.6.cloned.1.call-update) | async-done | bytes 262160 | tf_op jit(solution)/shard_map/while/body/eval_jaxpr/psum | solution.py:12
  182.3 1.0 pad_maximum_fusion.8
  183.3 1.2 fusion.63
  185.1 1.1 copy-done.2
  186.7 1.0 copy.37
  187.6 0.8 subtract_reduce_fusion.9
  189.5 1.3 collective-permute-start
  191.6 1.4 collective-permute-done
  192.9 32.6 %all-reduce.6.cloned.1.call-done = bf16[2,512,128]{2,1,0:T(8,128)(2,1)} async-done(((bf16[2,512,128]{2,1,0:T(8,128)(2,1)}), bf16[2,512,128]{2,1,0:T(8,128)(2,1)}) %all-reduce.6.cloned.1.call-update) | async-done | bytes 262160 | tf_op jit(solution)/shard_map/while/body/eval_jaxpr/psum | solution.py:12
  225.5 1.0 pad_maximum_fusion.8
  226.5 1.2 fusion.63
  228.3 1.1 copy-done.2
  229.9 1.0 copy.37
  230.9 0.8 subtract_reduce_fusion.9
  232.7 1.3 collective-permute-start
  234.8 1.4 collective-permute-done
  236.2 32.3 %all-reduce.6.cloned.1.call-done = bf16[2,512,128]{2,1,0:T(8,128)(2,1)} async-done(((bf16[2,512,128]{2,1,0:T(8,128)(2,1)}), bf16[2,512,128]{2,1,0:T(8,128)(2,1)}) %all-reduce.6.cloned.1.call-update) | async-done | bytes 262160 | tf_op jit(solution)/shard_map/while/body/eval_jaxpr/psum | solution.py:12
  268.4 1.0 pad_maximum_fusion.8
  269.4 1.2 fusion.63
  271.2 1.1 copy-done.2
  272.8 1.0 copy.37
  275.7 1.3 copy.19
  277.0 1.9 convolution_bitcast_fusion
  (100 shorter events, 16.5 us)
Async XLA Ops:
  8.0 130.2 %copy-start = (bf16[128,8192]{1,0:T(8,128)(2,1)S(1)}, bf16[128,8192]{1,0:T(8,128)(2,1)}, u32[]{:S(2)}) copy-start(bf16[128,8192]{1,0:T(8,128)(2,1)} %param.12) | copy-start | bytes 6291460
  8.0 130.2 %copy-start.11 = (bf16[512,128]{1,0:T(8,128)(2,1)S(1)}, bf16[512,128]{1,0:T(8,128)(2,1)}, u32[]{:S(2)}) copy-start(bf16[512,128]{1,0:T(8,128)(2,1)} %param.13) | copy-start | bytes 393220
  8.0 130.2 %all-gather.2.cloned.1.call-start = ((), (), s32[]{:S(2)}) async-start(), calls=%async_computation | async-start | bytes 9437184 | tf_op jit(solution)/shard_map/all_gather | solution.py:34
  8.8 135.2 %all-reduce.4.cloned.1.call-start = ((), (), s32[]{:S(2)}) async-start(), calls=%async_computation.1 | async-start | bytes 524288 | tf_op jit(solution)/shard_map/psum | solution.py:12
  13.9 0.6 copy-start.6
  14.6 130.4 %copy-start.3 = (bf16[256,128]{1,0:T(8,128)(2,1)}, bf16[256,128]{1,0:T(8,128)(2,1)S(1)}, u32[]{:S(2)}) copy-start(bf16[256,128]{1,0:T(8,128)(2,1)S(1)} %fusion.14) | copy-start | bytes 196612
  14.6 130.8 %copy-start.5 = (bf16[256,128]{1,0:T(8,128)(2,1)}, bf16[256,128]{1,0:T(8,128)(2,1)S(1)}, u32[]{:S(2)}) copy-start(bf16[256,128]{1,0:T(8,128)(2,1)S(1)} %subtract_convert_fusion) | copy-start | bytes 196612
  144.0 1.9 copy-start.9
  145.8 0.7 copy-start.10
  146.0 1.0 copy-start.1
  148.1 34.2 %all-reduce.6.cloned.1.call-start = ((), (), s32[]{:S(2)}) async-start(), calls=%async_computation.2 | async-start | bytes 524288 | tf_op jit(solution)/shard_map/while/body/eval_jaxpr/psum | solution.py:12
  148.1 3.5 %collective-permute-start = (bf16[512,128]{1,0:T(8,128)(2,1)}, bf16[512,128]{1,0:T(8,128)(2,1)S(1)}, u32[]{:S(2)}, u32[]{:S(2)}) collective-permute-start(bf16[512,128]{1,0:T(8,128)(2,1)} %get-tuple-element.535), channel_id=1, source_target_pairs={{8,0},{16,8},{24,16},{9,1},{17,9},{25,17},{10,2},{18,10},{26,18},{... | collective-permute-start | bytes 393224 | tf_op jit(solution)/shard_map/while/body/eval_jaxpr/ppermute | solution.py:18
  182.3 2.3 copy-start.4
  184.9 1.2 copy-start.2
  189.5 36.0 %all-reduce.6.cloned.1.call-start = ((), (), s32[]{:S(2)}) async-start(), calls=%async_computation.2 | async-start | bytes 524288 | tf_op jit(solution)/shard_map/while/body/eval_jaxpr/psum | solution.py:12
  189.5 3.4 %collective-permute-start = (bf16[512,128]{1,0:T(8,128)(2,1)}, bf16[512,128]{1,0:T(8,128)(2,1)S(1)}, u32[]{:S(2)}, u32[]{:S(2)}) collective-permute-start(bf16[512,128]{1,0:T(8,128)(2,1)} %get-tuple-element.535), channel_id=1, source_target_pairs={{8,0},{16,8},{24,16},{9,1},{17,9},{25,17},{10,2},{18,10},{26,18},{... | collective-permute-start | bytes 393224 | tf_op jit(solution)/shard_map/while/body/eval_jaxpr/ppermute | solution.py:18
  225.5 2.3 copy-start.4
  228.2 1.2 copy-start.2
  232.7 35.7 %all-reduce.6.cloned.1.call-start = ((), (), s32[]{:S(2)}) async-start(), calls=%async_computation.2 | async-start | bytes 524288 | tf_op jit(solution)/shard_map/while/body/eval_jaxpr/psum | solution.py:12
  232.7 3.4 %collective-permute-start = (bf16[512,128]{1,0:T(8,128)(2,1)}, bf16[512,128]{1,0:T(8,128)(2,1)S(1)}, u32[]{:S(2)}, u32[]{:S(2)}) collective-permute-start(bf16[512,128]{1,0:T(8,128)(2,1)} %get-tuple-element.535), channel_id=1, source_target_pairs={{8,0},{16,8},{24,16},{9,1},{17,9},{25,17},{10,2},{18,10},{26,18},{... | collective-permute-start | bytes 393224 | tf_op jit(solution)/shard_map/while/body/eval_jaxpr/ppermute | solution.py:18
  268.4 2.3 copy-start.4
  271.1 1.2 copy-start.2
  275.7 1.3 copy-start.7
  275.7 1.3 copy-start.8
Sparse Core Ops, SparseCore 0:
  11.0 127.1 all-gather.1
  151.8 30.4 all-reduce.5
  193.2 32.2 all-reduce.5
  236.1 32.2 all-reduce.5
Sparse Core Ops, SparseCore 1:
  12.1 34.7 all-reduce.3
where the time goes:
time: 288 us; the launch traced here: 287 us
  waiting for transfers between devices  224 us (78%)
  other arithmetic  17.4 us (6%)
  between operations  15.4 us (5%)
  matrix products  13.3 us (5%)
  local copies, waits for them, and re-layouts  13 us (5%)
  starting transfers between devices  3.98 us (1%)
    all_gather x1, waiting for transfers between devices, body(): lax.all_gather(d_out, 'chan', axis=1, tiled=True)  124 us
    psum x4, waiting for transfers between devices, spread(): return lax.psum(block, axis)  95.5 us
    while x18, local copies, waits for them, and re-layouts  8.26 us
  transfers between devices with their start and end apart: 8, of which 7 were waited for; matrix products, arithmetic and copies ran while one was open for 5% of the time, Pallas kernels for 0%

commit v1 on v0

--- a/solution.py
+++ b/solution.py
@@ -7,9 +7,15 @@
 SUBS = 4
 
 
+def gather_and_add(x, name):
+    blocks = lax.all_gather(x, name, axis=0, tiled=False)
+    total = blocks.sum(axis=0)
+    return total
+
+
 def spread(block, axis, holder):
     block = jnp.where(lax.axis_index(axis) == holder, block, jnp.zeros_like(block))
-    return lax.psum(block, axis)
+    return gather_and_add(block, axis)
 
 
 def shifted(block, axis, distance):

time: 288 us -> 257 us (0.89)
  waiting for transfers between devices: 224 us -> 190 us
    psum x4 -> x0, waiting for transfers between devices: 95.5 us -> none  [spread(): return lax.psum(block, axis)]
    all_gather x0 -> x4, waiting for transfers between devices: none -> 57.6 us  [gather_and_add(): blocks = lax.all_gather(x, name, axis=0, tiled=False)]
    reduce_sum x0 -> x4, other arithmetic: none -> 5.86 us  [gather_and_add(): total = blocks.sum(axis=0)]
    concatenate x4, other arithmetic: 4.06 us -> 0.15 us  [contribute(): spectra = transform(jnp.concatenate([grad_now[None], lag_pair], axis=0))]
    while x18 -> x30, local copies, waits for them, and re-layouts: 8.26 us -> 10.2 us
  transfers between devices with their start and end apart: 8 -> 8, of which waited for: 7 -> 8; matrix products, arithmetic and copies ran while one was open for 5% -> 3% of each run, Pallas kernels for 0% -> 0%
where the time goes in v1:
time: 257 us; the launch traced here: 256 us
  waiting for transfers between devices  190 us (74%)
  other arithmetic  19.7 us (8%)
  local copies, waits for them, and re-layouts  14.7 us (6%)
  between operations  14 us (5%)
  matrix products  13.3 us (5%)
  starting transfers between devices  4 us (2%)
    all_gather x1, waiting for transfers between devices, body(): lax.all_gather(d_out, 'chan', axis=1, tiled=True)  125 us
    all_gather x4, waiting for transfers between devices, gather_and_add(): blocks = lax.all_gather(x, name, axis=0, tiled=False)  57.6 us
    while x30, local copies, waits for them, and re-layouts  10.2 us
    ppermute x3, waiting for transfers between devices, shifted(): return lax.ppermute(block, axis, route)  6.39 us
    reduce_sum x4, other arithmetic, gather_and_add(): total = blocks.sum(axis=0)  5.86 us
    dot_general x1, matrix products, body(): jnp.einsum('td,cd->tc', lax.all_gather(d_out, 'chan', axis=1, tiled=True)...  5.71 us
  transfers between devices with their start and end apart: 8, of which 8 were waited for; matrix products, arithmetic and copies ran while one was open for 3% of the time, Pallas kernels for 0%

profile of v1, /device:TPU:0, one launch (start us, length us, event | category | flops | bytes accessed | tf_op | source)
XLA Modules:
  0.0 256.1 jit_solution(7900339329332616735)
XLA Ops:
  7.2 1.9 pad_maximum_fusion.4
  12.8 0.9 broadcast_multiply_fusion.1
  13.7 15.8 %all-gather.6.cloned.1.call-done = bf16[4,2,512,128]{3,2,1,0:T(8,128)(2,1)} async-done(((bf16[1,2,512,128]{3,2,1,0:T(8,128)(2,1)}), bf16[4,2,512,128]{3,2,1,0:T(8,128)(2,1)}) %all-gather.6.cloned.1.call-update) | async-done | bytes 1048592 | tf_op jit(solution)/shard_map/all_gather | solution.py:11
  29.6 1.5 reduce_sum.226
  31.0 125.2 %all-gather.4.cloned.1.call-done = bf16[512,8192]{1,0:T(8,128)(2,1)} async-done(((bf16[512,1024]{1,0:T(8,128)(2,1)}), bf16[512,8192]{1,0:T(8,128)(2,1)}) %all-gather.4.cloned.1.call-update) | async-done | bytes 8388624 | tf_op jit(solution)/shard_map/all_gather | solution.py:40
  156.3 5.7 %fusion.11 = bf16[512,128]{1,0:T(8,128)(2,1)S(1)} fusion(bf16[512,8192]{1,0:T(8,128)(2,1)} %all-gather.4.cloned.1.call-done, bf16[128,8192]{1,0:T(8,128)(2,1)S(1)} %copy-done, bf16[512,128]{1,0:T(8,128)(2,1)S(1)} %copy-done.13), kind=kOutput, calls=%fused_computation.46 | convolution fusion | flops 1073938432 | bytes 10747904 | tf_op jit(solution)/shard_map/td,cd->tc/dot_general | solution.py:38
  165.1 79.8 %while.23 = (s32[]{:T(128)}, bf16[512,128]{1,0:T(8,128)(2,1)}, f32[2,4,256,128]{2,3,1,0:T(8,128)}, f32[2,4,256,128]{2,3,0,1:T(8,128)S(1)}, bf16[1,2,512,128]{3,2...) while((s32[]{:T(128)}, bf16[512,128]{1,0:T(8,128)(2,1)}, ...), condition=%wide.region_19.20_spmd.clone.clone, body=%wide.region_9.19_spmd.clone.clone.sunk | while | flops 214237824 | bytes 42078560 | solution.py:116
  165.9 1.3 collective-permute-start
  167.2 2.1 collective-permute-done
  170.0 12.9 %all-gather.8.cloned.1.call-done = bf16[4,2,512,128]{3,2,1,0:T(8,128)(2,1)} async-done(((bf16[1,2,512,128]{3,2,1,0:T(8,128)(2,1)}), bf16[4,2,512,128]{3,2,1,0:T(8,128)(2,1)}) %all-gather.8.cloned.1.call-update) | async-done | bytes 1048592 | tf_op jit(solution)/shard_map/while/body/eval_jaxpr/all_gather | solution.py:11
  182.9 1.5 reduce_sum.272
  184.5 1.2 fusion.63
  186.3 1.1 copy-done.2
  187.8 1.0 copy.35
  188.8 0.8 subtract_reduce_fusion.9
  191.5 1.3 collective-permute-start
  192.8 2.1 collective-permute-done
  195.6 14.4 %all-gather.8.cloned.1.call-done = bf16[4,2,512,128]{3,2,1,0:T(8,128)(2,1)} async-done(((bf16[1,2,512,128]{3,2,1,0:T(8,128)(2,1)}), bf16[4,2,512,128]{3,2,1,0:T(8,128)(2,1)}) %all-gather.8.cloned.1.call-update) | async-done | bytes 1048592 | tf_op jit(solution)/shard_map/while/body/eval_jaxpr/all_gather | solution.py:11
  210.0 1.5 reduce_sum.272
  211.6 1.2 fusion.63
  213.4 1.1 copy-done.2
  214.9 1.0 copy.35
  215.9 0.8 subtract_reduce_fusion.9
  218.6 1.3 collective-permute-start
  219.9 2.1 collective-permute-done
  222.7 14.4 %all-gather.8.cloned.1.call-done = bf16[4,2,512,128]{3,2,1,0:T(8,128)(2,1)} async-done(((bf16[1,2,512,128]{3,2,1,0:T(8,128)(2,1)}), bf16[4,2,512,128]{3,2,1,0:T(8,128)(2,1)}) %all-gather.8.cloned.1.call-update) | async-done | bytes 1048592 | tf_op jit(solution)/shard_map/while/body/eval_jaxpr/all_gather | solution.py:11
  237.1 1.5 reduce_sum.272
  238.7 1.2 fusion.63
  240.5 1.1 copy-done.2
  242.0 1.0 copy.35
  244.9 1.3 copy.19
  246.2 1.9 convolution_bitcast_fusion
  (116 shorter events, 19.3 us)
Async XLA Ops:
  7.2 149.1 %copy-start = (bf16[128,8192]{1,0:T(8,128)(2,1)S(1)}, bf16[128,8192]{1,0:T(8,128)(2,1)}, u32[]{:S(2)}) copy-start(bf16[128,8192]{1,0:T(8,128)(2,1)} %param.12) | copy-start | bytes 6291460
  7.2 22.4 %all-gather.6.cloned.1.call-start = ((), (), s32[]{:S(2)}) async-start(), calls=%async_computation.1 | async-start | bytes 1310720 | tf_op jit(solution)/shard_map/all_gather | solution.py:11
  7.2 149.0 %copy-start.13 = (bf16[512,128]{1,0:T(8,128)(2,1)S(1)}, bf16[512,128]{1,0:T(8,128)(2,1)}, u32[]{:S(2)}) copy-start(bf16[512,128]{1,0:T(8,128)(2,1)} %param.13) | copy-start | bytes 393220
  9.1 147.1 %all-gather.4.cloned.1.call-start = ((), (), s32[]{:S(2)}) async-start(), calls=%async_computation | async-start | bytes 9437184 | tf_op jit(solution)/shard_map/all_gather | solution.py:40
  11.8 0.6 copy-start.8
  12.7 149.3 %copy-start.5 = (bf16[256,128]{1,0:T(8,128)(2,1)}, bf16[256,128]{1,0:T(8,128)(2,1)S(1)}, u32[]{:S(2)}) copy-start(bf16[256,128]{1,0:T(8,128)(2,1)S(1)} %fusion.14) | copy-start | bytes 196612
  13.7 148.7 %copy-start.7 = (bf16[256,128]{1,0:T(8,128)(2,1)}, bf16[256,128]{1,0:T(8,128)(2,1)S(1)}, u32[]{:S(2)}) copy-start(bf16[256,128]{1,0:T(8,128)(2,1)S(1)} %subtract_convert_fusion) | copy-start | bytes 196612
  162.0 0.9 copy-start.11
  162.9 0.7 copy-start.12
  163.0 1.0 copy-start.1
  165.1 5.0 %copy-start.3 = (bf16[1,2,512,128]{3,2,1,0:T(8,128)(2,1)}, bf16[1,2,512,128]{3,2,1,0:T(8,128)(2,1)S(1)}, u32[]{:S(2)}) copy-start(bf16[1,2,512,128]{3,2,1,0:T(8,128)(2,1)S(1)} %get-tuple-element.563) | copy-start | bytes 786436 | tf_op jit(solution)/shard_map/while
  165.1 17.9 %all-gather.8.cloned.1.call-start = ((), (), s32[]{:S(2)}) async-start(), calls=%async_computation.2 | async-start | bytes 1310720 | tf_op jit(solution)/shard_map/while/body/eval_jaxpr/all_gather | solution.py:11
  165.9 3.5 %collective-permute-start = (bf16[512,128]{1,0:T(8,128)(2,1)}, bf16[512,128]{1,0:T(8,128)(2,1)S(1)}, u32[]{:S(2)}, u32[]{:S(2)}) collective-permute-start(bf16[512,128]{1,0:T(8,128)(2,1)} %get-tuple-element.548), channel_id=1, source_target_pairs={{8,0},{16,8},{24,16},{9,1},{17,9},{25,17},{10,2},{18,10},{26,18},{... | collective-permute-start | bytes 393224 | tf_op jit(solution)/shard_map/while/body/eval_jaxpr/ppermute | solution.py:24
  184.4 1.3 copy-start.6
  186.1 1.2 copy-start.2
  189.7 1.0 copy-start.4
  190.7 4.9 %copy-start.3 = (bf16[1,2,512,128]{3,2,1,0:T(8,128)(2,1)}, bf16[1,2,512,128]{3,2,1,0:T(8,128)(2,1)S(1)}, u32[]{:S(2)}) copy-start(bf16[1,2,512,128]{3,2,1,0:T(8,128)(2,1)S(1)} %get-tuple-element.563) | copy-start | bytes 786436 | tf_op jit(solution)/shard_map/while
  190.7 19.4 %all-gather.8.cloned.1.call-start = ((), (), s32[]{:S(2)}) async-start(), calls=%async_computation.2 | async-start | bytes 1310720 | tf_op jit(solution)/shard_map/while/body/eval_jaxpr/all_gather | solution.py:11
  191.5 3.5 %collective-permute-start = (bf16[512,128]{1,0:T(8,128)(2,1)}, bf16[512,128]{1,0:T(8,128)(2,1)S(1)}, u32[]{:S(2)}, u32[]{:S(2)}) collective-permute-start(bf16[512,128]{1,0:T(8,128)(2,1)} %get-tuple-element.548), channel_id=1, source_target_pairs={{8,0},{16,8},{24,16},{9,1},{17,9},{25,17},{10,2},{18,10},{26,18},{... | collective-permute-start | bytes 393224 | tf_op jit(solution)/shard_map/while/body/eval_jaxpr/ppermute | solution.py:24
  211.5 1.3 copy-start.6
  213.2 1.2 copy-start.2
  216.8 1.0 copy-start.4
  217.8 4.9 %copy-start.3 = (bf16[1,2,512,128]{3,2,1,0:T(8,128)(2,1)}, bf16[1,2,512,128]{3,2,1,0:T(8,128)(2,1)S(1)}, u32[]{:S(2)}) copy-start(bf16[1,2,512,128]{3,2,1,0:T(8,128)(2,1)S(1)} %get-tuple-element.563) | copy-start | bytes 786436 | tf_op jit(solution)/shard_map/while
  217.8 19.4 %all-gather.8.cloned.1.call-start = ((), (), s32[]{:S(2)}) async-start(), calls=%async_computation.2 | async-start | bytes 1310720 | tf_op jit(solution)/shard_map/while/body/eval_jaxpr/all_gather | solution.py:11
  218.6 3.5 %collective-permute-start = (bf16[512,128]{1,0:T(8,128)(2,1)}, bf16[512,128]{1,0:T(8,128)(2,1)S(1)}, u32[]{:S(2)}, u32[]{:S(2)}) collective-permute-start(bf16[512,128]{1,0:T(8,128)(2,1)} %get-tuple-element.548), channel_id=1, source_target_pairs={{8,0},{16,8},{24,16},{9,1},{17,9},{25,17},{10,2},{18,10},{26,18},{... | collective-permute-start | bytes 393224 | tf_op jit(solution)/shard_map/while/body/eval_jaxpr/ppermute | solution.py:24
  238.6 1.3 copy-start.6
  240.3 1.2 copy-start.2
  243.9 1.0 copy-start.4
  244.9 1.3 copy-start.9
  244.9 1.3 copy-start.10
Sparse Core Ops, SparseCore 0:
  10.1 19.4 all-gather.5
  31.8 124.4 all-gather.3
  168.0 14.8 all-gather.7
  193.3 16.6 all-gather.7
  220.4 16.6 all-gather.7
